TPU v7x, 128 devices: a whole 4x4x4 slice. The times are simulated.
128 devices in a mesh: dp: 16 (over z, y_hi, core), seq: 8 (over x, y_lo).
Axes of the slice: x: 4, y: 4 (y_hi: 2, y_lo: 2; y = y_hi * 2 + y_lo), z: 4, core: 2. Of those that a mesh axis runs over, the one named last changes fastest.
Arguments:
- streams: bfloat16 [3, 16, 2048, 512], P(None, 'dp', 'seq'), may hold values from -6 to 6
- short_filter: float32 [3, 3, 512], replicated, may hold values from -3 to 3
- long_filter: float32 [2048, 512], P('seq'), may hold values from -4 to 4
- skip_gain: float32 [512], replicated, may hold values from -4 to 4
- out_weight: bfloat16 [512, 4096], replicated, may hold values from -0.25 to 0.25
- out_grad: bfloat16 [16, 2048, 4096], P('dp', 'seq'), may hold values from -6 to 6
Outputs:
- layer_out: bfloat16 [16, 2048, 4096], P('dp', 'seq')
- grad_streams: bfloat16 [3, 16, 2048, 512], P(None, 'dp', 'seq')
- grad_filter: float32 [2048, 512], P('seq')
- grad_out_weight: float32 [512, 4096], replicated
All inputs are finite; a program needn't handle non-finite values.
Results may differ from a plain program's by a relative error of at most 0.0049.
Values may be sent and summed in bfloat16 or wider, within the bound.
No kernel may reach another device: no remote copies, remote signals or barrier semaphores. Data moves between devices by JAX's collectives and lax.ppermute only.
A program may use at most 128 MiB of HBM per device.

v0:
```python
import math
import jax
import jax.numpy as jnp
from jax import lax
from jax.sharding import PartitionSpec as P


def swapped(array, axis, apart):
    return lax.ppermute(array, axis, [(i, i ^ 1 << apart) for i in range(lax.axis_size(axis))])


def passed_along(block, axis, distance):
    devices = range(lax.axis_size(axis))
    route = [(i - distance, i) for i in devices if i - distance in devices]
    return lax.ppermute(block, axis, route)


def spectral_table(length_here):
    row_index = lax.broadcasted_iota(jnp.int32, (length_here, length_here), 0)
    col_index = lax.broadcasted_iota(jnp.int32, (length_here, length_here), 1)
    phase_angle = (row_index * col_index % length_here).astype(jnp.float32) * (
        2.0 * math.pi / length_here
    )
    return (jnp.cos(phase_angle), jnp.sin(phase_angle))


def table_apply(matrix, values, pattern):
    return jnp.einsum(pattern, matrix, values, precision=lax.Precision.HIGHEST)


def transform_along(real_part, imaginary, direction, pattern):
    cosine, sine_table = spectral_table(real_part.shape[1])
    cosine_real = table_apply(cosine, real_part, pattern)
    cosine_imaginary = table_apply(cosine, imaginary, pattern)
    sine_real = table_apply(sine_table, real_part, pattern)
    sine_imaginary = table_apply(sine_table, imaginary, pattern)
    return (cosine_real - direction * sine_imaginary, cosine_imaginary + direction * sine_real)


def rotate_complex(real_part, imaginary, cosine, sine_value):
    return (
        real_part * cosine - imaginary * sine_value,
        real_part * sine_value + imaginary * cosine,
    )


def branch_angle(start_row, block_rows, total_length):
    positions = start_row + lax.broadcasted_iota(jnp.int32, (1, block_rows, 1), 1)
    return positions.astype(jnp.float32) * (math.pi / total_length)


def padded_branches(signal, start_row, total_length):
    phase_angle = branch_angle(start_row, signal.shape[1], total_length)
    real_part = jnp.concatenate([signal, signal * jnp.cos(phase_angle)], axis=0)
    imaginary = jnp.concatenate([jnp.zeros_like(signal), -signal * jnp.sin(phase_angle)], axis=0)
    return (real_part, imaginary)


def combine_branches(real_part, imaginary, start_row, total_length):
    members = real_part.shape[0] // 2
    phase_angle = branch_angle(start_row, real_part.shape[1], total_length)
    return 0.5 * (
        real_part[:members]
        + jnp.cos(phase_angle) * real_part[members:]
        - jnp.sin(phase_angle) * imaginary[members:]
    )


def level_twiddle(position, split_bit, block_rows):
    half_span = block_rows * (1 << split_bit)
    within = position % (1 << split_bit) * block_rows + lax.broadcasted_iota(
        jnp.int32, (1, block_rows, 1), 1
    )
    phase_angle = within.astype(jnp.float32) * (math.pi / half_span)
    return (jnp.cos(phase_angle), -jnp.sin(phase_angle))


def forward_levels(real_part, imaginary):
    seq_count = lax.axis_size("seq")
    position = lax.axis_index("seq")
    block_rows = real_part.shape[1]
    for split_bit in reversed(range(seq_count.bit_length() - 1)):
        upper_half = position >> split_bit & 1 == 1
        cosine, sine_value = level_twiddle(position, split_bit, block_rows)
        other_real, other_imaginary = swapped((real_part, imaginary), "seq", split_bit)
        turned_real, turned_imaginary = rotate_complex(
            other_real - real_part, other_imaginary - imaginary, cosine, sine_value
        )
        real_part = jnp.where(upper_half, turned_real, real_part + other_real)
        imaginary = jnp.where(upper_half, turned_imaginary, imaginary + other_imaginary)
    return (real_part, imaginary)


def inverse_levels(real_part, imaginary):
    seq_count = lax.axis_size("seq")
    position = lax.axis_index("seq")
    block_rows = real_part.shape[1]
    for split_bit in range(seq_count.bit_length() - 1):
        upper_half = position >> split_bit & 1 == 1
        cosine, sine_value = level_twiddle(position, split_bit, block_rows)
        turned_real, turned_imaginary = rotate_complex(real_part, imaginary, cosine, -sine_value)
        own_real = jnp.where(upper_half, turned_real, real_part)
        own_imaginary = jnp.where(upper_half, turned_imaginary, imaginary)
        other_real, other_imaginary = swapped((own_real, own_imaginary), "seq", split_bit)
        real_part = 0.5 * jnp.where(upper_half, other_real - own_real, other_real + own_real)
        imaginary = 0.5 * jnp.where(
            upper_half, other_imaginary - own_imaginary, other_imaginary + own_imaginary
        )
    return (real_part, imaginary)


def forward_spectrum(signal, start_row, total_length):
    real_part, imaginary = padded_branches(signal, start_row, total_length)
    real_part, imaginary = forward_levels(real_part, imaginary)
    return transform_along(real_part, imaginary, -1.0, "js,msc->mjc")


def inverse_signal(real_part, imaginary, start_row, total_length):
    block_rows = real_part.shape[1]
    real_part, imaginary = transform_along(real_part, imaginary, 1.0, "js,msc->mjc")
    real_part = real_part / block_rows
    imaginary = imaginary / block_rows
    real_part, imaginary = inverse_levels(real_part, imaginary)
    return combine_branches(real_part, imaginary, start_row, total_length)


def on_device(streams, short_filter, long_filter, skip_gain, out_weight, out_grad):
    seq_count = lax.axis_size("seq")
    batch_here = streams.shape[1]
    block_rows = streams.shape[2]
    channels = streams.shape[3]
    total_length = block_rows * seq_count
    start_row = lax.axis_index("seq") * block_rows
    grad_scale = 1.0 / math.sqrt(batch_here * lax.axis_size("dp") * total_length)
    earlier = passed_along(streams[:, :, block_rows - 2 :, :], "seq", 1)
    extended = jnp.concatenate([earlier, streams], axis=2).astype(jnp.float32)
    shortened = sum(
        (
            short_filter[:, offset, None, None, :]
            * extended[:, :, 2 - offset : 2 - offset + block_rows, :]
            for offset in range(3)
        )
    )
    gate_out, gate_in, value_stream = (shortened[0], shortened[1], shortened[2])
    product = gate_in * value_stream
    members = batch_here + 1
    spectrum_real, spectrum_imaginary = forward_spectrum(
        jnp.concatenate([product, long_filter[None]], axis=0), start_row, total_length
    )
    spectrum_real = spectrum_real.reshape(2, members, block_rows, channels)
    spectrum_imaginary = spectrum_imaginary.reshape(2, members, block_rows, channels)
    product_real, product_imaginary = (
        spectrum_real[:, :batch_here],
        spectrum_imaginary[:, :batch_here],
    )
    filter_real, filter_imaginary = (
        spectrum_real[:, batch_here:],
        spectrum_imaginary[:, batch_here:],
    )
    conv_real = product_real * filter_real - product_imaginary * filter_imaginary
    conv_imaginary = product_real * filter_imaginary + product_imaginary * filter_real
    convolved = inverse_signal(
        conv_real.reshape(2 * batch_here, block_rows, channels),
        conv_imaginary.reshape(2 * batch_here, block_rows, channels),
        start_row,
        total_length,
    )
    convolved = convolved + skip_gain * product
    mixed_out = (gate_out * convolved).astype(jnp.bfloat16)
    mixed_flat = mixed_out.reshape(batch_here * block_rows, channels)
    grad_flat = out_grad.reshape(batch_here * block_rows, out_grad.shape[2])
    layer_out = (
        jnp.dot(mixed_flat, out_weight, preferred_element_type=jnp.float32)
        .astype(jnp.bfloat16)
        .reshape(out_grad.shape)
    )
    grad_mixed = lax.dot_general(
        grad_flat, out_weight, (((1,), (1,)), ((), ())), preferred_element_type=jnp.float32
    ).reshape(batch_here, block_rows, channels)
    grad_conv = grad_mixed * gate_out
    grad_gate_out = grad_mixed * convolved
    grad_real, grad_imaginary = forward_spectrum(grad_conv, start_row, total_length)
    grad_real = grad_real.reshape(2, batch_here, block_rows, channels)
    grad_imaginary = grad_imaginary.reshape(2, batch_here, block_rows, channels)
    back_real = filter_real * grad_real + filter_imaginary * grad_imaginary
    back_imaginary = filter_real * grad_imaginary - filter_imaginary * grad_real
    lag_real = jnp.sum(
        product_real * grad_real + product_imaginary * grad_imaginary, axis=1, keepdims=True
    )
    lag_imaginary = jnp.sum(
        product_real * grad_imaginary - product_imaginary * grad_real, axis=1, keepdims=True
    )
    joined_real = jnp.concatenate([back_real, lag_real], axis=1).reshape(
        2 * members, block_rows, channels
    )
    joined_imaginary = jnp.concatenate([back_imaginary, lag_imaginary], axis=1).reshape(
        2 * members, block_rows, channels
    )
    inverse_rows = inverse_signal(joined_real, joined_imaginary, start_row, total_length)
    grad_product = inverse_rows[:batch_here] + skip_gain * grad_conv
    filter_part = inverse_rows[batch_here]
    grad_shortened = jnp.stack([grad_gate_out, grad_product * value_stream, grad_product * gate_in])
    later_rows = passed_along(grad_shortened[:, :, :2, :], "seq", -1)
    extended_grad = jnp.concatenate([grad_shortened, later_rows], axis=2)
    grad_streams = sum(
        (
            short_filter[:, offset, None, None, :]
            * extended_grad[:, :, offset : offset + block_rows, :]
            for offset in range(3)
        )
    )
    partial_value = lax.dot_general(
        mixed_flat, grad_flat, (((0,), (0,)), ((), ())), preferred_element_type=jnp.float32
    )
    grad_out_weight = lax.psum(partial_value, ("dp", "seq")) * grad_scale
    grad_filter = lax.psum(filter_part, "dp") * grad_scale
    return (layer_out, grad_streams.astype(jnp.bfloat16), grad_filter, grad_out_weight)


def solution(mesh):
    placed = (P(None, "dp", "seq", None), P(), P("seq", None), P(), P(), P("dp", "seq", None))
    return jax.shard_map(
        on_device,
        mesh=mesh,
        in_specs=placed,
        out_specs=(P("dp", "seq", None), P(None, "dp", "seq", None), P("seq", None), P()),
        check_vma=False,
    )
```

profile of v0, /device:TPU:1, one launch (start us, length us, event | category | flops | bytes accessed | tf_op | source)
XLA Modules:
  0.0 1175.4 jit_solution(6477687003662021271)
XLA Ops:
  8.1 4.0 collective-permute-start
  13.2 1.4 maximum_convert_fusion
  15.8 1.5 pad_maximum_fusion
  17.5 3.8 collective-permute-start.1
  21.3 1.6 concatenate.47
  26.8 2.6 collective-permute-start.13
  31.0 34.8 %collective-permute-done.1 = f32[4,256,512]{2,1,0:T(8,128)} collective-permute-done((f32[4,256,512]{2,1,0:T(8,128)}, f32[4,256,512]{2,1,0:T(8,128)}, u32[]{:S(2)}, u32[]{:S(2)}) %collective-permute-start.1) | collective-permute-done | bytes 2097184 | tf_op jit(solution)/shard_map/ppermute | solution.py:9
  65.7 44.9 %collective-permute-done.2 = f32[4,256,512]{2,1,0:T(8,128)} collective-permute-done((f32[4,256,512]{2,1,0:T(8,128)}, f32[4,256,512]{2,1,0:T(8,128)}, u32[]{:S(2)}, u32[]{:S(2)}) %collective-permute-start.2) | collective-permute-done | bytes 2097184 | tf_op jit(solution)/shard_map/ppermute | solution.py:9
  110.7 6.2 add_select_fusion.9
  118.4 14.8 %collective-permute-done.13 = f32[2,256,512]{2,1,0:T(8,128)} collective-permute-done((f32[2,256,512]{2,1,0:T(8,128)}, f32[2,256,512]{2,1,0:T(8,128)}, u32[]{:S(2)}, u32[]{:S(2)}) %collective-permute-start.13) | collective-permute-done | bytes 1048608 | tf_op jit(solution)/shard_map/ppermute | solution.py:9
  133.1 22.5 %collective-permute-done.14 = f32[2,256,512]{2,1,0:T(8,128)} collective-permute-done((f32[2,256,512]{2,1,0:T(8,128)}, f32[2,256,512]{2,1,0:T(8,128)}, u32[]{:S(2)}, u32[]{:S(2)}) %collective-permute-start.14) | collective-permute-done | bytes 1048608 | tf_op jit(solution)/shard_map/ppermute | solution.py:9
  155.6 3.5 add_select_fusion.14
  160.6 107.4 %collective-permute-done.15 = f32[2,256,512]{2,1,0:T(8,128)} collective-permute-done((f32[2,256,512]{2,1,0:T(8,128)}, f32[2,256,512]{2,1,0:T(8,128)}, u32[]{:S(2)}, u32[]{:S(2)}) %collective-permute-start.15) | collective-permute-done | bytes 1048608 | tf_op jit(solution)/shard_map/ppermute | solution.py:9
  268.0 22.5 %collective-permute-done.16 = f32[2,256,512]{2,1,0:T(8,128)} collective-permute-done((f32[2,256,512]{2,1,0:T(8,128)}, f32[2,256,512]{2,1,0:T(8,128)}, u32[]{:S(2)}, u32[]{:S(2)}) %collective-permute-start.16) | collective-permute-done | bytes 1048608 | tf_op jit(solution)/shard_map/ppermute | solution.py:9
  290.5 4.1 add_select_fusion.12
  296.1 6.7 add_select_fusion.7
  303.1 1.6 collective-permute-start.6
  304.8 12.0 %collective-permute-done.17 = f32[2,256,512]{2,1,0:T(8,128)} collective-permute-done((f32[2,256,512]{2,1,0:T(8,128)}, f32[2,256,512]{2,1,0:T(8,128)}, u32[]{:S(2)}, u32[]{:S(2)}) %collective-permute-start.17) | collective-permute-done | bytes 1048608 | tf_op jit(solution)/shard_map/ppermute | solution.py:9
  316.8 22.5 %collective-permute-done.18 = f32[2,256,512]{2,1,0:T(8,128)} collective-permute-done((f32[2,256,512]{2,1,0:T(8,128)}, f32[2,256,512]{2,1,0:T(8,128)}, u32[]{:S(2)}, u32[]{:S(2)}) %collective-permute-start.18) | collective-permute-done | bytes 1048608 | tf_op jit(solution)/shard_map/ppermute | solution.py:9
  339.3 2.7 add_select_fusion.10
  342.0 2.7 convolution_multiply_fusion
  344.7 2.7 fusion.10
  347.4 2.7 convolution_multiply_fusion.1
  350.0 34.2 %collective-permute-done.5 = f32[4,256,512]{2,1,0:T(8,128)} collective-permute-done((f32[4,256,512]{2,1,0:T(8,128)}, f32[4,256,512]{2,1,0:T(8,128)}, u32[]{:S(2)}, u32[]{:S(2)}) %collective-permute-start.5) | collective-permute-done | bytes 2097184 | tf_op jit(solution)/shard_map/ppermute | solution.py:9
  384.2 44.9 %collective-permute-done.6 = f32[4,256,512]{2,1,0:T(8,128)} collective-permute-done((f32[4,256,512]{2,1,0:T(8,128)}, f32[4,256,512]{2,1,0:T(8,128)}, u32[]{:S(2)}, u32[]{:S(2)}) %collective-permute-start.6) | collective-permute-done | bytes 2097184 | tf_op jit(solution)/shard_map/ppermute | solution.py:9
  429.2 4.6 add_select_fusion.5
  433.8 4.7 fusion.39
  438.5 4.5 fusion.41
  443.0 4.5 multiply_add_fusion
  447.5 4.9 multiply_subtract_fusion
  452.4 6.3 multiply_subtract_fusion.2
  458.7 1.5 pad_maximum_fusion.1
  460.2 2.9 copy.42
  463.1 3.0 pad_maximum_fusion.2
  466.1 2.9 copy.43
  469.0 4.8 fusion.43
  473.8 3.1 fusion.45
  476.9 3.3 convolution_add_fusion
  480.2 4.0 select_bitcast_fusion
  485.9 2.1 fusion.15
  488.0 2.1 fusion.19
  490.0 2.1 convolution_add_fusion.2
  492.1 35.7 %collective-permute-done.19 = f32[4,256,512]{2,1,0:T(8,128)S(1)} collective-permute-done((f32[4,256,512]{2,1,0:T(8,128)S(1)}, f32[4,256,512]{2,1,0:T(8,128)S(1)}, u32[]{:S(2)}, u32[]{:S(2)}) %collective-permute-start.19) | collective-permute-done | bytes 2097184 | tf_op jit(solution)/shard_map/ppermute | solution.py:9
  527.8 44.9 %collective-permute-done.20 = f32[4,256,512]{2,1,0:T(8,128)S(1)} collective-permute-done((f32[4,256,512]{2,1,0:T(8,128)S(1)}, f32[4,256,512]{2,1,0:T(8,128)S(1)}, u32[]{:S(2)}, u32[]{:S(2)}) %collective-permute-start.20) | collective-permute-done | bytes 2097184 | tf_op jit(solution)/shard_map/ppermute | solution.py:9
  572.7 1.5 multiply_select_fusion.2
  576.0 2.5 select_bitcast_fusion.2
  580.0 18.0 %collective-permute-done.7 = f32[2,256,512]{2,1,0:T(8,128)S(1)} collective-permute-done((f32[2,256,512]{2,1,0:T(8,128)S(1)}, f32[2,256,512]{2,1,0:T(8,128)S(1)}, u32[]{:S(2)}, u32[]{:S(2)}) %collective-permute-start.7) | collective-permute-done | bytes 1048608 | tf_op jit(solution)/shard_map/ppermute | solution.py:9
  598.0 22.5 %collective-permute-done.8 = f32[2,256,512]{2,1,0:T(8,128)S(1)} collective-permute-done((f32[2,256,512]{2,1,0:T(8,128)S(1)}, f32[2,256,512]{2,1,0:T(8,128)S(1)}, u32[]{:S(2)}, u32[]{:S(2)}) %collective-permute-start.8) | collective-permute-done | bytes 1048608 | tf_op jit(solution)/shard_map/ppermute | solution.py:9
  622.7 39.0 %collective-permute-done.22 = f32[4,256,512]{2,1,0:T(8,128)S(1)} collective-permute-done((f32[4,256,512]{2,1,0:T(8,128)S(1)}, f32[4,256,512]{2,1,0:T(8,128)S(1)}, u32[]{:S(2)}, u32[]{:S(2)}) %collective-permute-start.22) | collective-permute-done | bytes 2097184 | tf_op jit(solution)/shard_map/ppermute | solution.py:9
  661.8 1.5 multiply_select_fusion
  663.3 1.8 collective-permute-start.23
  666.3 17.9 %collective-permute-done.10 = f32[2,256,512]{2,1,0:T(8,128)S(1)} collective-permute-done((f32[2,256,512]{2,1,0:T(8,128)S(1)}, f32[2,256,512]{2,1,0:T(8,128)S(1)}, u32[]{:S(2)}, u32[]{:S(2)}) %collective-permute-start.10) | collective-permute-done | bytes 1048608 | tf_op jit(solution)/shard_map/ppermute | solution.py:9
  684.2 22.5 %collective-permute-done.9 = f32[2,256,512]{2,1,0:T(8,128)S(1)} collective-permute-done((f32[2,256,512]{2,1,0:T(8,128)S(1)}, f32[2,256,512]{2,1,0:T(8,128)S(1)}, u32[]{:S(2)}, u32[]{:S(2)}) %collective-permute-start.9) | collective-permute-done | bytes 1048608 | tf_op jit(solution)/shard_map/ppermute | solution.py:9
  707.4 1.8 collective-permute-start.11
  710.5 109.4 %collective-permute-done.11 = f32[2,256,512]{2,1,0:T(8,128)S(1)} collective-permute-done((f32[2,256,512]{2,1,0:T(8,128)S(1)}, f32[2,256,512]{2,1,0:T(8,128)S(1)}, u32[]{:S(2)}, u32[]{:S(2)}) %collective-permute-start.11) | collective-permute-done | bytes 1048608 | tf_op jit(solution)/shard_map/ppermute | solution.py:9
  820.2 22.2 %collective-permute-done.12 = f32[2,256,512]{2,1,0:T(8,128)S(1)} collective-permute-done((f32[2,256,512]{2,1,0:T(8,128)S(1)}, f32[2,256,512]{2,1,0:T(8,128)S(1)}, u32[]{:S(2)}, u32[]{:S(2)}) %collective-permute-start.12) | collective-permute-done | bytes 1048608 | tf_op jit(solution)/shard_map/ppermute | solution.py:9
  845.8 4.7 fusion.1
  852.8 1.7 collective-permute-start.25
  854.5 4.8 fusion
  859.4 1.4 fusion.6
  860.8 130.1 %all-reduce.5.cloned.1.call-done = f32[256,512]{1,0:T(8,128)} async-done(((f32[256,512]{1,0:T(8,128)}), f32[256,512]{1,0:T(8,128)}) %all-reduce.5.cloned.1.call-update) | async-done | bytes 524304 | tf_op jit(solution)/shard_map/psum | solution.py:216
  990.9 1.9 broadcast_multiply_fusion.1
  992.7 167.3 %all-reduce.7.cloned.1.call-done = f32[512,4096]{1,0:T(8,128)} async-done(((f32[512,4096]{1,0:T(8,128)}), f32[512,4096]{1,0:T(8,128)}) %all-reduce.7.cloned.1.call-update) | async-done | bytes 8388624 | tf_op jit(solution)/shard_map/psum | solution.py:215
  1160.1 8.3 broadcast_multiply_fusion
  (100 shorter events, 30.0 us)
Async XLA Ops:
  7.2 16.1 %copy-start = (bf16[1,256,4096]{2,1,0:T(8,128)(2,1)S(1)}, bf16[1,256,4096]{2,1,0:T(8,128)(2,1)}, u32[]{:S(2)}) copy-start(bf16[1,256,4096]{2,1,0:T(8,128)(2,1)} %param.11) | copy-start | bytes 6291460
  7.2 983.7 %all-reduce.5.cloned.1.call-start = ((), (), s32[]{:S(2)}) async-start(), calls=%async_computation | async-start | bytes 1048576 | tf_op jit(solution)/shard_map/psum | solution.py:216
  8.1 5.0 collective-permute-start
  14.5 1.0 copy-start.11
  15.0 9.6 copy-start.1
  15.8 1.7 copy-start.6
  15.8 5.5 copy-start.5
  15.8 7.5 copy-start.19
  17.5 48.2 %collective-permute-start.1 = (f32[4,256,512]{2,1,0:T(8,128)}, f32[4,256,512]{2,1,0:T(8,128)}, u32[]{:S(2)}, u32[]{:S(2)}) collective-permute-start(f32[4,256,512]{2,1,0:T(8,128)} %pad_maximum_fusion), channel_id=1, source_target_pairs={{0,4},{1,5},{2,6},{3,7},{4,0},{5,1},{6,2},{7,3},{8,12},{9,13},{10,... | collective-permute-start | bytes 6291464 | tf_op jit(solution)/shard_map/ppermute | solution.py:9
  22.9 87.8 %collective-permute-start.2 = (f32[4,256,512]{2,1,0:T(8,128)}, f32[4,256,512]{2,1,0:T(8,128)}, u32[]{:S(2)}, u32[]{:S(2)}) collective-permute-start(f32[4,256,512]{2,1,0:T(8,128)} %concatenate.47), channel_id=1, source_target_pairs={{0,4},{1,5},{2,6},{3,7},{4,0},{5,1},{6,2},{7,3},{8,12},{9,13},{10,... | collective-permute-start | bytes 6291464 | tf_op jit(solution)/shard_map/ppermute | solution.py:9
  24.6 2.2 copy-start.16
  24.7 5.8 copy-start.14
  24.9 0.9 copy-start.12
  26.8 106.3 %collective-permute-start.13 = (f32[2,256,512]{2,1,0:T(8,128)}, f32[2,256,512]{2,1,0:T(8,128)}, u32[]{:S(2)}, u32[]{:S(2)}) collective-permute-start(f32[2,256,512]{2,1,0:T(8,128)} %pad_maximum_fusion.6), channel_id=1, source_target_pairs={{0,4},{1,5},{2,6},{3,7},{4,0},{5,1},{6,2},{7,3},{8,12},{9,13},{10,... | collective-permute-start | bytes 3145736 | tf_op jit(solution)/shard_map/ppermute | solution.py:9
  30.5 125.1 %collective-permute-start.14 = (f32[2,256,512]{2,1,0:T(8,128)}, f32[2,256,512]{2,1,0:T(8,128)}, u32[]{:S(2)}, u32[]{:S(2)}) collective-permute-start(f32[2,256,512]{2,1,0:T(8,128)} %concatenate.49), channel_id=1, source_target_pairs={{0,4},{1,5},{2,6},{3,7},{4,0},{5,1},{6,2},{7,3},{8,12},{9,13},{10,... | collective-permute-start | bytes 3145736 | tf_op jit(solution)/shard_map/ppermute | solution.py:9
  110.7 44.9 %copy-start.13 = (f32[1,256,512]{2,1,0:T(8,128)S(1)}, f32[1,256,512]{2,1,0:T(8,128)}, u32[]{:S(2)}) copy-start(f32[1,256,512]{2,1,0:T(8,128)} %copy-done.12) | copy-start | bytes 1572868
  110.7 44.9 %copy-start.15 = (f32[1,256,512]{2,1,0:T(8,128)S(1)}, f32[1,256,512]{2,1,0:T(8,128)}, u32[]{:S(2)}) copy-start(f32[1,256,512]{2,1,0:T(8,128)} %copy-done.14) | copy-start | bytes 1572868
  116.9 179.2 %collective-permute-start.3 = (f32[4,256,512]{2,1,0:T(8,128)}, f32[4,256,512]{2,1,0:T(8,128)}, u32[]{:S(2)}, u32[]{:S(2)}) collective-permute-start(f32[4,256,512]{2,1,0:T(8,128)} %get-tuple-element.16), channel_id=1, source_target_pairs={{0,2},{1,3},{2,0},{3,1},{4,6},{5,7},{6,4},{7,5},{8,10},{9,11},{10,... | collective-permute-start | bytes 6291464 | tf_op jit(solution)/shard_map/ppermute | solution.py:9
  118.0 178.0 %collective-permute-start.4 = (f32[4,256,512]{2,1,0:T(8,128)}, f32[4,256,512]{2,1,0:T(8,128)}, u32[]{:S(2)}, u32[]{:S(2)}) collective-permute-start(f32[4,256,512]{2,1,0:T(8,128)} %get-tuple-element.17), channel_id=1, source_target_pairs={{0,2},{1,3},{2,0},{3,1},{4,6},{5,7},{6,4},{7,5},{8,10},{9,11},{10,... | collective-permute-start | bytes 6291464 | tf_op jit(solution)/shard_map/ppermute | solution.py:9
  159.1 108.9 %collective-permute-start.15 = (f32[2,256,512]{2,1,0:T(8,128)}, f32[2,256,512]{2,1,0:T(8,128)}, u32[]{:S(2)}, u32[]{:S(2)}) collective-permute-start(f32[2,256,512]{2,1,0:T(8,128)} %get-tuple-element.35), channel_id=1, source_target_pairs={{0,2},{1,3},{2,0},{3,1},{4,6},{5,7},{6,4},{7,5},{8,10},{9,11},{10,... | collective-permute-start | bytes 3145736 | tf_op jit(solution)/shard_map/ppermute | solution.py:9
  160.2 130.2 %collective-permute-start.16 = (f32[2,256,512]{2,1,0:T(8,128)}, f32[2,256,512]{2,1,0:T(8,128)}, u32[]{:S(2)}, u32[]{:S(2)}) collective-permute-start(f32[2,256,512]{2,1,0:T(8,128)} %get-tuple-element.34), channel_id=1, source_target_pairs={{0,2},{1,3},{2,0},{3,1},{4,6},{5,7},{6,4},{7,5},{8,10},{9,11},{10,... | collective-permute-start | bytes 3145736 | tf_op jit(solution)/shard_map/ppermute | solution.py:9
  294.6 22.2 %collective-permute-start.17 = (f32[2,256,512]{2,1,0:T(8,128)}, f32[2,256,512]{2,1,0:T(8,128)}, u32[]{:S(2)}, u32[]{:S(2)}) collective-permute-start(f32[2,256,512]{2,1,0:T(8,128)} %get-tuple-element.27), channel_id=1, source_target_pairs={{0,1},{1,0},{2,3},{3,2},{4,5},{5,4},{6,7},{7,6},{8,9},{9,8},{10,11... | collective-permute-start | bytes 3145736 | tf_op jit(solution)/shard_map/ppermute | solution.py:9
  295.0 44.3 %collective-permute-start.18 = (f32[2,256,512]{2,1,0:T(8,128)}, f32[2,256,512]{2,1,0:T(8,128)}, u32[]{:S(2)}, u32[]{:S(2)}) collective-permute-start(f32[2,256,512]{2,1,0:T(8,128)} %get-tuple-element.26), channel_id=1, source_target_pairs={{0,1},{1,0},{2,3},{3,2},{4,5},{5,4},{6,7},{7,6},{8,9},{9,8},{10,11... | collective-permute-start | bytes 3145736 | tf_op jit(solution)/shard_map/ppermute | solution.py:9
  302.7 81.5 %collective-permute-start.5 = (f32[4,256,512]{2,1,0:T(8,128)}, f32[4,256,512]{2,1,0:T(8,128)}, u32[]{:S(2)}, u32[]{:S(2)}) collective-permute-start(f32[4,256,512]{2,1,0:T(8,128)} %get-tuple-element.14), channel_id=1, source_target_pairs={{0,1},{1,0},{2,3},{3,2},{4,5},{5,4},{6,7},{7,6},{8,9},{9,8},{10,11... | collective-permute-start | bytes 6291464 | tf_op jit(solution)/shard_map/ppermute | solution.py:9
  303.1 126.0 %collective-permute-start.6 = (f32[4,256,512]{2,1,0:T(8,128)}, f32[4,256,512]{2,1,0:T(8,128)}, u32[]{:S(2)}, u32[]{:S(2)}) collective-permute-start(f32[4,256,512]{2,1,0:T(8,128)} %get-tuple-element.15), channel_id=1, source_target_pairs={{0,1},{1,0},{2,3},{3,2},{4,5},{5,4},{6,7},{7,6},{8,9},{9,8},{10,11... | collective-permute-start | bytes 6291464 | tf_op jit(solution)/shard_map/ppermute | solution.py:9
  469.0 4.8 copy-start.3
  476.9 3.3 copy-start.4
  480.2 5.6 copy-start.7
  484.3 3.7 copy-start.8
  484.3 43.5 %collective-permute-start.19 = (f32[4,256,512]{2,1,0:T(8,128)S(1)}, f32[4,256,512]{2,1,0:T(8,128)S(1)}, u32[]{:S(2)}, u32[]{:S(2)}) collective-permute-start(f32[4,256,512]{2,1,0:T(8,128)S(1)} %get-tuple-element.23), channel_id=1, source_target_pairs={{0,1},{1,0},{2,3},{3,2},{4,5},{5,4},{6,7},{7,6},{8,9},{9,8},{10,11... | collective-permute-start | bytes 6291464 | tf_op jit(solution)/shard_map/ppermute | solution.py:9
  484.7 88.0 %collective-permute-start.20 = (f32[4,256,512]{2,1,0:T(8,128)S(1)}, f32[4,256,512]{2,1,0:T(8,128)S(1)}, u32[]{:S(2)}, u32[]{:S(2)}) collective-permute-start(f32[4,256,512]{2,1,0:T(8,128)S(1)} %get-tuple-element.22), channel_id=1, source_target_pairs={{0,1},{1,0},{2,3},{3,2},{4,5},{5,4},{6,7},{7,6},{8,9},{9,8},{10,11... | collective-permute-start | bytes 6291464 | tf_op jit(solution)/shard_map/ppermute | solution.py:9
  574.2 48.5 %collective-permute-start.21 = (f32[4,256,512]{2,1,0:T(8,128)S(1)}, f32[4,256,512]{2,1,0:T(8,128)S(1)}, u32[]{:S(2)}, u32[]{:S(2)}) collective-permute-start(f32[4,256,512]{2,1,0:T(8,128)S(1)} %get-tuple-element.11), channel_id=1, source_target_pairs={{0,2},{1,3},{2,0},{3,1},{4,6},{5,7},{6,4},{7,5},{8,10},{9,11},{10,... | collective-permute-start | bytes 6291464 | tf_op jit(solution)/shard_map/ppermute | solution.py:9
  575.5 86.3 %collective-permute-start.22 = (f32[4,256,512]{2,1,0:T(8,128)S(1)}, f32[4,256,512]{2,1,0:T(8,128)S(1)}, u32[]{:S(2)}, u32[]{:S(2)}) collective-permute-start(f32[4,256,512]{2,1,0:T(8,128)S(1)} %get-tuple-element.10), channel_id=1, source_target_pairs={{0,2},{1,3},{2,0},{3,1},{4,6},{5,7},{6,4},{7,5},{8,10},{9,11},{10,... | collective-permute-start | bytes 6291464 | tf_op jit(solution)/shard_map/ppermute | solution.py:9
  578.4 19.6 %collective-permute-start.7 = (f32[2,256,512]{2,1,0:T(8,128)S(1)}, f32[2,256,512]{2,1,0:T(8,128)S(1)}, u32[]{:S(2)}, u32[]{:S(2)}) collective-permute-start(f32[2,256,512]{2,1,0:T(8,128)S(1)} %get-tuple-element.39), channel_id=1, source_target_pairs={{0,1},{1,0},{2,3},{3,2},{4,5},{5,4},{6,7},{7,6},{8,9},{9,8},{10,11... | collective-permute-start | bytes 3145736 | tf_op jit(solution)/shard_map/ppermute | solution.py:9
  578.9 41.6 %collective-permute-start.8 = (f32[2,256,512]{2,1,0:T(8,128)S(1)}, f32[2,256,512]{2,1,0:T(8,128)S(1)}, u32[]{:S(2)}, u32[]{:S(2)}) collective-permute-start(f32[2,256,512]{2,1,0:T(8,128)S(1)} %get-tuple-element.38), channel_id=1, source_target_pairs={{0,1},{1,0},{2,3},{3,2},{4,5},{5,4},{6,7},{7,6},{8,9},{9,8},{10,11... | collective-permute-start | bytes 3145736 | tf_op jit(solution)/shard_map/ppermute | solution.py:9
  621.1 63.1 %collective-permute-start.10 = (f32[2,256,512]{2,1,0:T(8,128)S(1)}, f32[2,256,512]{2,1,0:T(8,128)S(1)}, u32[]{:S(2)}, u32[]{:S(2)}) collective-permute-start(f32[2,256,512]{2,1,0:T(8,128)S(1)} %get-tuple-element.30), channel_id=1, source_target_pairs={{0,2},{1,3},{2,0},{3,1},{4,6},{5,7},{6,4},{7,5},{8,10},{9,11},{10,... | collective-permute-start | bytes 3145736 | tf_op jit(solution)/shard_map/ppermute | solution.py:9
  622.4 84.3 %collective-permute-start.9 = (f32[2,256,512]{2,1,0:T(8,128)S(1)}, f32[2,256,512]{2,1,0:T(8,128)S(1)}, u32[]{:S(2)}, u32[]{:S(2)}) collective-permute-start(f32[2,256,512]{2,1,0:T(8,128)S(1)} %get-tuple-element.31), channel_id=1, source_target_pairs={{0,2},{1,3},{2,0},{3,1},{4,6},{5,7},{6,4},{7,5},{8,10},{9,11},{10,... | collective-permute-start | bytes 3145736 | tf_op jit(solution)/shard_map/ppermute | solution.py:9
  663.3 180.2 %collective-permute-start.23 = (f32[4,256,512]{2,1,0:T(8,128)S(1)}, f32[4,256,512]{2,1,0:T(8,128)S(1)}, u32[]{:S(2)}, u32[]{:S(2)}) collective-permute-start(f32[4,256,512]{2,1,0:T(8,128)S(1)} %get-tuple-element.9), channel_id=1, source_target_pairs={{0,4},{1,5},{2,6},{3,7},{4,0},{5,1},{6,2},{7,3},{8,12},{9,13},{10,... | collective-permute-start | bytes 6291464 | tf_op jit(solution)/shard_map/ppermute | solution.py:9
  665.1 178.9 %collective-permute-start.24 = (f32[4,256,512]{2,1,0:T(8,128)S(1)}, f32[4,256,512]{2,1,0:T(8,128)S(1)}, u32[]{:S(2)}, u32[]{:S(2)}) collective-permute-start(f32[4,256,512]{2,1,0:T(8,128)S(1)} %get-tuple-element.8), channel_id=1, source_target_pairs={{0,4},{1,5},{2,6},{3,7},{4,0},{5,1},{6,2},{7,3},{8,12},{9,13},{10,... | collective-permute-start | bytes 6291464 | tf_op jit(solution)/shard_map/ppermute | solution.py:9
  707.4 135.0 %copy-start.2 = (f32[3,1,256,512]{3,2,1,0:T(8,128)S(1)}, f32[3,1,256,512]{3,2,1,0:T(8,128)}, u32[]{:S(2)}) copy-start(f32[3,1,256,512]{3,2,1,0:T(8,128)} %copy-done.1) | copy-start | bytes 4718596
  707.4 135.0 %copy-start.17 = (f32[256,512]{1,0:T(8,128)S(1)}, f32[256,512]{1,0:T(8,128)}, u32[]{:S(2)}) copy-start(f32[256,512]{1,0:T(8,128)} %copy-done.16) | copy-start | bytes 1572868
  707.4 135.0 %copy-start.18 = (f32[512]{0:T(512)S(1)}, f32[512]{0:T(512)}, u32[]{:S(2)}) copy-start(f32[512]{0:T(512)} %param.9) | copy-start | bytes 6148
  707.4 112.5 %collective-permute-start.11 = (f32[2,256,512]{2,1,0:T(8,128)S(1)}, f32[2,256,512]{2,1,0:T(8,128)S(1)}, u32[]{:S(2)}, u32[]{:S(2)}) collective-permute-start(f32[2,256,512]{2,1,0:T(8,128)S(1)} %get-tuple-element.28), channel_id=1, source_target_pairs={{0,4},{1,5},{2,6},{3,7},{4,0},{5,1},{6,2},{7,3},{8,12},{9,13},{10,... | collective-permute-start | bytes 3145736 | tf_op jit(solution)/shard_map/ppermute | solution.py:9
  709.2 133.1 %collective-permute-start.12 = (f32[2,256,512]{2,1,0:T(8,128)S(1)}, f32[2,256,512]{2,1,0:T(8,128)S(1)}, u32[]{:S(2)}, u32[]{:S(2)}) collective-permute-start(f32[2,256,512]{2,1,0:T(8,128)S(1)} %get-tuple-element.29), channel_id=1, source_target_pairs={{0,4},{1,5},{2,6},{3,7},{4,0},{5,1},{6,2},{7,3},{8,12},{9,13},{10,... | collective-permute-start | bytes 3145736 | tf_op jit(solution)/shard_map/ppermute | solution.py:9
  845.8 314.3 %all-reduce.7.cloned.1.call-start = ((), (), s32[]{:S(2)}) async-start(), calls=%async_computation.1 | async-start | bytes 16777216 | tf_op jit(solution)/shard_map/psum | solution.py:215
  850.5 1.0 copy-start.9
  852.8 6.5 copy-start.10
  852.8 6.5 collective-permute-start.25
Sparse Core Ops, SparseCore 0:
  845.9 144.8 all-reduce.4
  997.3 162.7 all-reduce.6
where the time goes:
time: 1180 us
  waiting for transfers between devices  990 us (84%)
  matrix products  67.5 us (6%)
  other arithmetic  58.3 us (5%)
  starting transfers between devices  31.8 us (3%)
  between operations  14.8 us (1%)
  local copies, waits for them, and re-layouts  12.9 us (1%)
    ppermute x24, waiting for transfers between devices, swapped(): lax.ppermute(array, axis, [(i, i ^ 1 << apart) for i in range(lax.axis_si...  693 us
    psum x1, waiting for transfers between devices, on_device(): grad_out_weight = lax.psum(partial_value, ('dp', 'seq')) * grad_scale  167 us
    psum x1, waiting for transfers between devices, on_device(): grad_filter = lax.psum(filter_part, 'dp') * grad_scale  130 us
    dot_general x16, matrix products, table_apply(): return jnp.einsum(pattern, matrix, values, precision=lax.Precision.HIGHEST)  56.8 us
    ppermute x24, starting transfers between devices, swapped(): lax.ppermute(array, axis, [(i, i ^ 1 << apart) for i in range(lax.axis_si...  26 us
  transfers between devices with their start and end apart: 28, of which 21 were waited for; matrix products, arithmetic and copies ran while one was open for 6% of the time, Pallas kernels for 0%

commit v1 on v0

--- a/solution.py
+++ b/solution.py
@@ -212,7 +212,7 @@
     partial_value = lax.dot_general(
         mixed_flat, grad_flat, (((0,), (0,)), ((), ())), preferred_element_type=jnp.float32
     )
-    grad_out_weight = lax.psum(partial_value, ("dp", "seq")) * grad_scale
+    grad_out_weight = lax.psum(lax.psum(partial_value, "dp"), "seq") * grad_scale
     grad_filter = lax.psum(filter_part, "dp") * grad_scale
     return (layer_out, grad_streams.astype(jnp.bfloat16), grad_filter, grad_out_weight)
 

time: 1180 us -> 1430 us (1.21)
  waiting for transfers between devices: 990 us -> 1240 us
    psum x1, waiting for transfers between devices: 167 us -> 330 us  [on_device(): lax.psum(lax.psum(partial_value, 'dp'), 'seq') * grad_scale]
    psum x1, waiting for transfers between devices: 130 us -> 213 us  [on_device(): grad_filter = lax.psum(filter_part, 'dp') * grad_scale]
  transfers between devices with their start and end apart: 28 -> 28, of which waited for: 21 -> 21; matrix products, arithmetic and copies ran while one was open for 6% -> 4% of each run, Pallas kernels for 0% -> 0%
where the time goes in v1:
time: 1430 us; the launch traced here: 1420 us
  waiting for transfers between devices  1240 us (87%)
  matrix products  67.5 us (5%)
  other arithmetic  57.2 us (4%)
  starting transfers between devices  31.8 us (2%)
  between operations  14.8 us (1%)
    ppermute x24, waiting for transfers between devices, swapped(): lax.ppermute(array, axis, [(i, i ^ 1 << apart) for i in range(lax.axis_si...  693 us
    psum x1, waiting for transfers between devices, on_device(): lax.psum(lax.psum(partial_value, 'dp'), 'seq') * grad_scale  330 us
    psum x1, waiting for transfers between devices, on_device(): grad_filter = lax.psum(filter_part, 'dp') * grad_scale  213 us
    dot_general x16, matrix products, table_apply(): return jnp.einsum(pattern, matrix, values, precision=lax.Precision.HIGHEST)  56.8 us
  transfers between devices with their start and end apart: 28, of which 21 were waited for; matrix products, arithmetic and copies ran while one was open for 4% of the time, Pallas kernels for 0%

profile of v1, /device:TPU:1, one launch (start us, length us, event | category | flops | bytes accessed | tf_op | source)
XLA Modules:
  0.0 1420.1 jit_solution(14657721365988845128)
XLA Ops:
  8.1 4.0 collective-permute-start
  13.2 1.4 maximum_convert_fusion
  15.8 1.5 pad_maximum_fusion
  17.5 3.8 collective-permute-start.1
  21.3 1.6 concatenate.47
  26.8 2.5 collective-permute-start.13
  30.9 34.8 %collective-permute-done.1 = f32[4,256,512]{2,1,0:T(8,128)} collective-permute-done((f32[4,256,512]{2,1,0:T(8,128)}, f32[4,256,512]{2,1,0:T(8,128)}, u32[]{:S(2)}, u32[]{:S(2)}) %collective-permute-start.1) | collective-permute-done | bytes 2097184 | tf_op jit(solution)/shard_map/ppermute | solution.py:9
  65.7 44.9 %collective-permute-done.2 = f32[4,256,512]{2,1,0:T(8,128)} collective-permute-done((f32[4,256,512]{2,1,0:T(8,128)}, f32[4,256,512]{2,1,0:T(8,128)}, u32[]{:S(2)}, u32[]{:S(2)}) %collective-permute-start.2) | collective-permute-done | bytes 2097184 | tf_op jit(solution)/shard_map/ppermute | solution.py:9
  110.7 6.2 add_select_fusion.9
  118.3 14.8 %collective-permute-done.13 = f32[2,256,512]{2,1,0:T(8,128)} collective-permute-done((f32[2,256,512]{2,1,0:T(8,128)}, f32[2,256,512]{2,1,0:T(8,128)}, u32[]{:S(2)}, u32[]{:S(2)}) %collective-permute-start.13) | collective-permute-done | bytes 1048608 | tf_op jit(solution)/shard_map/ppermute | solution.py:9
  133.1 22.5 %collective-permute-done.14 = f32[2,256,512]{2,1,0:T(8,128)} collective-permute-done((f32[2,256,512]{2,1,0:T(8,128)}, f32[2,256,512]{2,1,0:T(8,128)}, u32[]{:S(2)}, u32[]{:S(2)}) %collective-permute-start.14) | collective-permute-done | bytes 1048608 | tf_op jit(solution)/shard_map/ppermute | solution.py:9
  155.6 3.4 add_select_fusion.14
  160.6 107.4 %collective-permute-done.15 = f32[2,256,512]{2,1,0:T(8,128)} collective-permute-done((f32[2,256,512]{2,1,0:T(8,128)}, f32[2,256,512]{2,1,0:T(8,128)}, u32[]{:S(2)}, u32[]{:S(2)}) %collective-permute-start.15) | collective-permute-done | bytes 1048608 | tf_op jit(solution)/shard_map/ppermute | solution.py:9
  268.0 22.5 %collective-permute-done.16 = f32[2,256,512]{2,1,0:T(8,128)} collective-permute-done((f32[2,256,512]{2,1,0:T(8,128)}, f32[2,256,512]{2,1,0:T(8,128)}, u32[]{:S(2)}, u32[]{:S(2)}) %collective-permute-start.16) | collective-permute-done | bytes 1048608 | tf_op jit(solution)/shard_map/ppermute | solution.py:9
  290.5 4.1 add_select_fusion.12
  296.0 6.7 add_select_fusion.7
  303.1 1.6 collective-permute-start.6
  304.8 12.0 collective-permute-done.17
  316.8 22.5 %collective-permute-done.18 = f32[2,256,512]{2,1,0:T(8,128)} collective-permute-done((f32[2,256,512]{2,1,0:T(8,128)}, f32[2,256,512]{2,1,0:T(8,128)}, u32[]{:S(2)}, u32[]{:S(2)}) %collective-permute-start.18) | collective-permute-done | bytes 1048608 | tf_op jit(solution)/shard_map/ppermute | solution.py:9
  339.3 2.7 add_select_fusion.10
  342.0 2.7 convolution_multiply_fusion
  344.7 2.7 fusion.10
  347.3 2.7 convolution_multiply_fusion.1
  350.0 34.2 %collective-permute-done.5 = f32[4,256,512]{2,1,0:T(8,128)} collective-permute-done((f32[4,256,512]{2,1,0:T(8,128)}, f32[4,256,512]{2,1,0:T(8,128)}, u32[]{:S(2)}, u32[]{:S(2)}) %collective-permute-start.5) | collective-permute-done | bytes 2097184 | tf_op jit(solution)/shard_map/ppermute | solution.py:9
  384.2 44.9 %collective-permute-done.6 = f32[4,256,512]{2,1,0:T(8,128)} collective-permute-done((f32[4,256,512]{2,1,0:T(8,128)}, f32[4,256,512]{2,1,0:T(8,128)}, u32[]{:S(2)}, u32[]{:S(2)}) %collective-permute-start.6) | collective-permute-done | bytes 2097184 | tf_op jit(solution)/shard_map/ppermute | solution.py:9
  429.1 4.6 add_select_fusion.5
  433.8 4.7 fusion.39
  438.5 4.5 fusion.41
  443.0 4.5 multiply_add_fusion
  447.5 4.9 multiply_subtract_fusion
  452.4 6.3 multiply_subtract_fusion.2
  458.7 1.5 pad_maximum_fusion.1
  460.2 2.9 copy.42
  463.1 3.0 pad_maximum_fusion.2
  466.1 2.9 copy.43
  469.0 4.8 fusion.43
  473.8 3.1 fusion.45
  476.9 3.3 convolution_add_fusion
  480.2 4.0 select_bitcast_fusion
  485.9 2.1 fusion.15
  487.9 2.1 fusion.19
  490.0 2.1 convolution_add_fusion.2
  492.1 35.7 %collective-permute-done.19 = f32[4,256,512]{2,1,0:T(8,128)S(1)} collective-permute-done((f32[4,256,512]{2,1,0:T(8,128)S(1)}, f32[4,256,512]{2,1,0:T(8,128)S(1)}, u32[]{:S(2)}, u32[]{:S(2)}) %collective-permute-start.19) | collective-permute-done | bytes 2097184 | tf_op jit(solution)/shard_map/ppermute | solution.py:9
  527.8 44.9 %collective-permute-done.20 = f32[4,256,512]{2,1,0:T(8,128)S(1)} collective-permute-done((f32[4,256,512]{2,1,0:T(8,128)S(1)}, f32[4,256,512]{2,1,0:T(8,128)S(1)}, u32[]{:S(2)}, u32[]{:S(2)}) %collective-permute-start.20) | collective-permute-done | bytes 2097184 | tf_op jit(solution)/shard_map/ppermute | solution.py:9
  572.7 1.5 multiply_select_fusion.2
  576.0 2.5 select_bitcast_fusion.2
  580.0 18.0 %collective-permute-done.7 = f32[2,256,512]{2,1,0:T(8,128)S(1)} collective-permute-done((f32[2,256,512]{2,1,0:T(8,128)S(1)}, f32[2,256,512]{2,1,0:T(8,128)S(1)}, u32[]{:S(2)}, u32[]{:S(2)}) %collective-permute-start.7) | collective-permute-done | bytes 1048608 | tf_op jit(solution)/shard_map/ppermute | solution.py:9
  598.0 22.5 %collective-permute-done.8 = f32[2,256,512]{2,1,0:T(8,128)S(1)} collective-permute-done((f32[2,256,512]{2,1,0:T(8,128)S(1)}, f32[2,256,512]{2,1,0:T(8,128)S(1)}, u32[]{:S(2)}, u32[]{:S(2)}) %collective-permute-start.8) | collective-permute-done | bytes 1048608 | tf_op jit(solution)/shard_map/ppermute | solution.py:9
  622.8 39.0 %collective-permute-done.22 = f32[4,256,512]{2,1,0:T(8,128)S(1)} collective-permute-done((f32[4,256,512]{2,1,0:T(8,128)S(1)}, f32[4,256,512]{2,1,0:T(8,128)S(1)}, u32[]{:S(2)}, u32[]{:S(2)}) %collective-permute-start.22) | collective-permute-done | bytes 2097184 | tf_op jit(solution)/shard_map/ppermute | solution.py:9
  661.8 1.5 multiply_select_fusion
  663.3 1.8 collective-permute-start.23
  666.3 17.9 %collective-permute-done.10 = f32[2,256,512]{2,1,0:T(8,128)S(1)} collective-permute-done((f32[2,256,512]{2,1,0:T(8,128)S(1)}, f32[2,256,512]{2,1,0:T(8,128)S(1)}, u32[]{:S(2)}, u32[]{:S(2)}) %collective-permute-start.10) | collective-permute-done | bytes 1048608 | tf_op jit(solution)/shard_map/ppermute | solution.py:9
  684.3 22.5 %collective-permute-done.9 = f32[2,256,512]{2,1,0:T(8,128)S(1)} collective-permute-done((f32[2,256,512]{2,1,0:T(8,128)S(1)}, f32[2,256,512]{2,1,0:T(8,128)S(1)}, u32[]{:S(2)}, u32[]{:S(2)}) %collective-permute-start.9) | collective-permute-done | bytes 1048608 | tf_op jit(solution)/shard_map/ppermute | solution.py:9
  707.4 1.8 collective-permute-start.11
  710.5 109.4 %collective-permute-done.11 = f32[2,256,512]{2,1,0:T(8,128)S(1)} collective-permute-done((f32[2,256,512]{2,1,0:T(8,128)S(1)}, f32[2,256,512]{2,1,0:T(8,128)S(1)}, u32[]{:S(2)}, u32[]{:S(2)}) %collective-permute-start.11) | collective-permute-done | bytes 1048608 | tf_op jit(solution)/shard_map/ppermute | solution.py:9
  820.2 22.2 %collective-permute-done.12 = f32[2,256,512]{2,1,0:T(8,128)S(1)} collective-permute-done((f32[2,256,512]{2,1,0:T(8,128)S(1)}, f32[2,256,512]{2,1,0:T(8,128)S(1)}, u32[]{:S(2)}, u32[]{:S(2)}) %collective-permute-start.12) | collective-permute-done | bytes 1048608 | tf_op jit(solution)/shard_map/ppermute | solution.py:9
  844.4 1.4 multiply_bitcast_fusion.1
  845.8 4.7 fusion.1
  850.5 212.8 %all-reduce.8.cloned.1.call-done = (f32[256,512]{1,0:T(8,128)}, f32[512,4096]{1,0:T(8,128)}) async-done(((f32[256,512]{1,0:T(8,128)}, f32[512,4096]{1,0:T(8,128)}), (f32[256,512]{1,0:T(8,128)}, f32[512,4096]{1,0:T(8,128)})) %all-reduce.8.cloned.1.call-update) | async-done | bytes 8912912 | tf_op jit(solution)/shard_map/psum | solution.py:216
  1065.6 1.7 collective-permute-start.25
  1067.3 4.8 fusion
  1072.2 1.4 fusion.6
  1074.5 330.3 %all-reduce.6.cloned.1.call-done = f32[512,4096]{1,0:T(8,128)} async-done(((f32[512,4096]{1,0:T(8,128)}), f32[512,4096]{1,0:T(8,128)}) %all-reduce.6.cloned.1.call-update) | async-done | bytes 8388624 | tf_op jit(solution)/shard_map/psum | solution.py:215
  1404.7 8.3 broadcast_multiply_fusion
  (102 shorter events, 29.6 us)
Async XLA Ops:
  7.2 16.1 %copy-start = (bf16[1,256,4096]{2,1,0:T(8,128)(2,1)S(1)}, bf16[1,256,4096]{2,1,0:T(8,128)(2,1)}, u32[]{:S(2)}) copy-start(bf16[1,256,4096]{2,1,0:T(8,128)(2,1)} %param.11) | copy-start | bytes 6291460
  7.2 1056.2 %all-reduce.8.cloned.1.call-start = ((), (), s32[]{:S(2)}) async-start(), calls=%async_computation.1 | async-start | bytes 17825792 | tf_op jit(solution)/shard_map/psum | solution.py:216
  8.1 5.0 collective-permute-start
  14.5 1.0 copy-start.11
  15.0 9.6 copy-start.1
  15.8 1.7 copy-start.6
  15.8 5.5 copy-start.5
  15.8 7.5 copy-start.20
  17.5 48.2 %collective-permute-start.1 = (f32[4,256,512]{2,1,0:T(8,128)}, f32[4,256,512]{2,1,0:T(8,128)}, u32[]{:S(2)}, u32[]{:S(2)}) collective-permute-start(f32[4,256,512]{2,1,0:T(8,128)} %pad_maximum_fusion), channel_id=1, source_target_pairs={{0,4},{1,5},{2,6},{3,7},{4,0},{5,1},{6,2},{7,3},{8,12},{9,13},{10,... | collective-permute-start | bytes 6291464 | tf_op jit(solution)/shard_map/ppermute | solution.py:9
  22.9 87.8 %collective-permute-start.2 = (f32[4,256,512]{2,1,0:T(8,128)}, f32[4,256,512]{2,1,0:T(8,128)}, u32[]{:S(2)}, u32[]{:S(2)}) collective-permute-start(f32[4,256,512]{2,1,0:T(8,128)} %concatenate.47), channel_id=1, source_target_pairs={{0,4},{1,5},{2,6},{3,7},{4,0},{5,1},{6,2},{7,3},{8,12},{9,13},{10,... | collective-permute-start | bytes 6291464 | tf_op jit(solution)/shard_map/ppermute | solution.py:9
  24.6 2.2 copy-start.16
  24.7 5.7 copy-start.14
  24.9 0.9 copy-start.12
  26.8 106.3 %collective-permute-start.13 = (f32[2,256,512]{2,1,0:T(8,128)}, f32[2,256,512]{2,1,0:T(8,128)}, u32[]{:S(2)}, u32[]{:S(2)}) collective-permute-start(f32[2,256,512]{2,1,0:T(8,128)} %pad_maximum_fusion.6), channel_id=1, source_target_pairs={{0,4},{1,5},{2,6},{3,7},{4,0},{5,1},{6,2},{7,3},{8,12},{9,13},{10,... | collective-permute-start | bytes 3145736 | tf_op jit(solution)/shard_map/ppermute | solution.py:9
  30.4 125.2 %collective-permute-start.14 = (f32[2,256,512]{2,1,0:T(8,128)}, f32[2,256,512]{2,1,0:T(8,128)}, u32[]{:S(2)}, u32[]{:S(2)}) collective-permute-start(f32[2,256,512]{2,1,0:T(8,128)} %concatenate.49), channel_id=1, source_target_pairs={{0,4},{1,5},{2,6},{3,7},{4,0},{5,1},{6,2},{7,3},{8,12},{9,13},{10,... | collective-permute-start | bytes 3145736 | tf_op jit(solution)/shard_map/ppermute | solution.py:9
  110.7 44.9 %copy-start.13 = (f32[1,256,512]{2,1,0:T(8,128)S(1)}, f32[1,256,512]{2,1,0:T(8,128)}, u32[]{:S(2)}) copy-start(f32[1,256,512]{2,1,0:T(8,128)} %copy-done.12) | copy-start | bytes 1572868
  110.7 44.9 %copy-start.15 = (f32[1,256,512]{2,1,0:T(8,128)S(1)}, f32[1,256,512]{2,1,0:T(8,128)}, u32[]{:S(2)}) copy-start(f32[1,256,512]{2,1,0:T(8,128)} %copy-done.14) | copy-start | bytes 1572868
  116.9 179.2 %collective-permute-start.3 = (f32[4,256,512]{2,1,0:T(8,128)}, f32[4,256,512]{2,1,0:T(8,128)}, u32[]{:S(2)}, u32[]{:S(2)}) collective-permute-start(f32[4,256,512]{2,1,0:T(8,128)} %get-tuple-element.18), channel_id=1, source_target_pairs={{0,2},{1,3},{2,0},{3,1},{4,6},{5,7},{6,4},{7,5},{8,10},{9,11},{10,... | collective-permute-start | bytes 6291464 | tf_op jit(solution)/shard_map/ppermute | solution.py:9
  118.0 178.0 %collective-permute-start.4 = (f32[4,256,512]{2,1,0:T(8,128)}, f32[4,256,512]{2,1,0:T(8,128)}, u32[]{:S(2)}, u32[]{:S(2)}) collective-permute-start(f32[4,256,512]{2,1,0:T(8,128)} %get-tuple-element.19), channel_id=1, source_target_pairs={{0,2},{1,3},{2,0},{3,1},{4,6},{5,7},{6,4},{7,5},{8,10},{9,11},{10,... | collective-permute-start | bytes 6291464 | tf_op jit(solution)/shard_map/ppermute | solution.py:9
  159.0 109.0 %collective-permute-start.15 = (f32[2,256,512]{2,1,0:T(8,128)}, f32[2,256,512]{2,1,0:T(8,128)}, u32[]{:S(2)}, u32[]{:S(2)}) collective-permute-start(f32[2,256,512]{2,1,0:T(8,128)} %get-tuple-element.37), channel_id=1, source_target_pairs={{0,2},{1,3},{2,0},{3,1},{4,6},{5,7},{6,4},{7,5},{8,10},{9,11},{10,... | collective-permute-start | bytes 3145736 | tf_op jit(solution)/shard_map/ppermute | solution.py:9
  160.2 130.3 %collective-permute-start.16 = (f32[2,256,512]{2,1,0:T(8,128)}, f32[2,256,512]{2,1,0:T(8,128)}, u32[]{:S(2)}, u32[]{:S(2)}) collective-permute-start(f32[2,256,512]{2,1,0:T(8,128)} %get-tuple-element.36), channel_id=1, source_target_pairs={{0,2},{1,3},{2,0},{3,1},{4,6},{5,7},{6,4},{7,5},{8,10},{9,11},{10,... | collective-permute-start | bytes 3145736 | tf_op jit(solution)/shard_map/ppermute | solution.py:9
  294.6 22.2 %collective-permute-start.17 = (f32[2,256,512]{2,1,0:T(8,128)}, f32[2,256,512]{2,1,0:T(8,128)}, u32[]{:S(2)}, u32[]{:S(2)}) collective-permute-start(f32[2,256,512]{2,1,0:T(8,128)} %get-tuple-element.29), channel_id=1, source_target_pairs={{0,1},{1,0},{2,3},{3,2},{4,5},{5,4},{6,7},{7,6},{8,9},{9,8},{10,11... | collective-permute-start | bytes 3145736 | tf_op jit(solution)/shard_map/ppermute | solution.py:9
  295.0 44.3 %collective-permute-start.18 = (f32[2,256,512]{2,1,0:T(8,128)}, f32[2,256,512]{2,1,0:T(8,128)}, u32[]{:S(2)}, u32[]{:S(2)}) collective-permute-start(f32[2,256,512]{2,1,0:T(8,128)} %get-tuple-element.28), channel_id=1, source_target_pairs={{0,1},{1,0},{2,3},{3,2},{4,5},{5,4},{6,7},{7,6},{8,9},{9,8},{10,11... | collective-permute-start | bytes 3145736 | tf_op jit(solution)/shard_map/ppermute | solution.py:9
  302.7 81.5 %collective-permute-start.5 = (f32[4,256,512]{2,1,0:T(8,128)}, f32[4,256,512]{2,1,0:T(8,128)}, u32[]{:S(2)}, u32[]{:S(2)}) collective-permute-start(f32[4,256,512]{2,1,0:T(8,128)} %get-tuple-element.16), channel_id=1, source_target_pairs={{0,1},{1,0},{2,3},{3,2},{4,5},{5,4},{6,7},{7,6},{8,9},{9,8},{10,11... | collective-permute-start | bytes 6291464 | tf_op jit(solution)/shard_map/ppermute | solution.py:9
  303.1 126.0 %collective-permute-start.6 = (f32[4,256,512]{2,1,0:T(8,128)}, f32[4,256,512]{2,1,0:T(8,128)}, u32[]{:S(2)}, u32[]{:S(2)}) collective-permute-start(f32[4,256,512]{2,1,0:T(8,128)} %get-tuple-element.17), channel_id=1, source_target_pairs={{0,1},{1,0},{2,3},{3,2},{4,5},{5,4},{6,7},{7,6},{8,9},{9,8},{10,11... | collective-permute-start | bytes 6291464 | tf_op jit(solution)/shard_map/ppermute | solution.py:9
  469.0 4.8 copy-start.3
  476.9 3.3 copy-start.4
  480.2 5.6 copy-start.7
  484.2 3.7 copy-start.8
  484.3 43.5 %collective-permute-start.19 = (f32[4,256,512]{2,1,0:T(8,128)S(1)}, f32[4,256,512]{2,1,0:T(8,128)S(1)}, u32[]{:S(2)}, u32[]{:S(2)}) collective-permute-start(f32[4,256,512]{2,1,0:T(8,128)S(1)} %get-tuple-element.25), channel_id=1, source_target_pairs={{0,1},{1,0},{2,3},{3,2},{4,5},{5,4},{6,7},{7,6},{8,9},{9,8},{10,11... | collective-permute-start | bytes 6291464 | tf_op jit(solution)/shard_map/ppermute | solution.py:9
  484.7 88.0 %collective-permute-start.20 = (f32[4,256,512]{2,1,0:T(8,128)S(1)}, f32[4,256,512]{2,1,0:T(8,128)S(1)}, u32[]{:S(2)}, u32[]{:S(2)}) collective-permute-start(f32[4,256,512]{2,1,0:T(8,128)S(1)} %get-tuple-element.24), channel_id=1, source_target_pairs={{0,1},{1,0},{2,3},{3,2},{4,5},{5,4},{6,7},{7,6},{8,9},{9,8},{10,11... | collective-permute-start | bytes 6291464 | tf_op jit(solution)/shard_map/ppermute | solution.py:9
  574.2 48.5 %collective-permute-start.21 = (f32[4,256,512]{2,1,0:T(8,128)S(1)}, f32[4,256,512]{2,1,0:T(8,128)S(1)}, u32[]{:S(2)}, u32[]{:S(2)}) collective-permute-start(f32[4,256,512]{2,1,0:T(8,128)S(1)} %get-tuple-element.13), channel_id=1, source_target_pairs={{0,2},{1,3},{2,0},{3,1},{4,6},{5,7},{6,4},{7,5},{8,10},{9,11},{10,... | collective-permute-start | bytes 6291464 | tf_op jit(solution)/shard_map/ppermute | solution.py:9
  575.4 86.4 %collective-permute-start.22 = (f32[4,256,512]{2,1,0:T(8,128)S(1)}, f32[4,256,512]{2,1,0:T(8,128)S(1)}, u32[]{:S(2)}, u32[]{:S(2)}) collective-permute-start(f32[4,256,512]{2,1,0:T(8,128)S(1)} %get-tuple-element.12), channel_id=1, source_target_pairs={{0,2},{1,3},{2,0},{3,1},{4,6},{5,7},{6,4},{7,5},{8,10},{9,11},{10,... | collective-permute-start | bytes 6291464 | tf_op jit(solution)/shard_map/ppermute | solution.py:9
  578.4 19.6 %collective-permute-start.7 = (f32[2,256,512]{2,1,0:T(8,128)S(1)}, f32[2,256,512]{2,1,0:T(8,128)S(1)}, u32[]{:S(2)}, u32[]{:S(2)}) collective-permute-start(f32[2,256,512]{2,1,0:T(8,128)S(1)} %get-tuple-element.41), channel_id=1, source_target_pairs={{0,1},{1,0},{2,3},{3,2},{4,5},{5,4},{6,7},{7,6},{8,9},{9,8},{10,11... | collective-permute-start | bytes 3145736 | tf_op jit(solution)/shard_map/ppermute | solution.py:9
  578.9 41.6 %collective-permute-start.8 = (f32[2,256,512]{2,1,0:T(8,128)S(1)}, f32[2,256,512]{2,1,0:T(8,128)S(1)}, u32[]{:S(2)}, u32[]{:S(2)}) collective-permute-start(f32[2,256,512]{2,1,0:T(8,128)S(1)} %get-tuple-element.40), channel_id=1, source_target_pairs={{0,1},{1,0},{2,3},{3,2},{4,5},{5,4},{6,7},{7,6},{8,9},{9,8},{10,11... | collective-permute-start | bytes 3145736 | tf_op jit(solution)/shard_map/ppermute | solution.py:9
  621.2 63.1 %collective-permute-start.10 = (f32[2,256,512]{2,1,0:T(8,128)S(1)}, f32[2,256,512]{2,1,0:T(8,128)S(1)}, u32[]{:S(2)}, u32[]{:S(2)}) collective-permute-start(f32[2,256,512]{2,1,0:T(8,128)S(1)} %get-tuple-element.32), channel_id=1, source_target_pairs={{0,2},{1,3},{2,0},{3,1},{4,6},{5,7},{6,4},{7,5},{8,10},{9,11},{10,... | collective-permute-start | bytes 3145736 | tf_op jit(solution)/shard_map/ppermute | solution.py:9
  622.3 84.4 %collective-permute-start.9 = (f32[2,256,512]{2,1,0:T(8,128)S(1)}, f32[2,256,512]{2,1,0:T(8,128)S(1)}, u32[]{:S(2)}, u32[]{:S(2)}) collective-permute-start(f32[2,256,512]{2,1,0:T(8,128)S(1)} %get-tuple-element.33), channel_id=1, source_target_pairs={{0,2},{1,3},{2,0},{3,1},{4,6},{5,7},{6,4},{7,5},{8,10},{9,11},{10,... | collective-permute-start | bytes 3145736 | tf_op jit(solution)/shard_map/ppermute | solution.py:9
  663.3 180.2 %collective-permute-start.23 = (f32[4,256,512]{2,1,0:T(8,128)S(1)}, f32[4,256,512]{2,1,0:T(8,128)S(1)}, u32[]{:S(2)}, u32[]{:S(2)}) collective-permute-start(f32[4,256,512]{2,1,0:T(8,128)S(1)} %get-tuple-element.11), channel_id=1, source_target_pairs={{0,4},{1,5},{2,6},{3,7},{4,0},{5,1},{6,2},{7,3},{8,12},{9,13},{10,... | collective-permute-start | bytes 6291464 | tf_op jit(solution)/shard_map/ppermute | solution.py:9
  665.1 179.0 %collective-permute-start.24 = (f32[4,256,512]{2,1,0:T(8,128)S(1)}, f32[4,256,512]{2,1,0:T(8,128)S(1)}, u32[]{:S(2)}, u32[]{:S(2)}) collective-permute-start(f32[4,256,512]{2,1,0:T(8,128)S(1)} %get-tuple-element.10), channel_id=1, source_target_pairs={{0,4},{1,5},{2,6},{3,7},{4,0},{5,1},{6,2},{7,3},{8,12},{9,13},{10,... | collective-permute-start | bytes 6291464 | tf_op jit(solution)/shard_map/ppermute | solution.py:9
  707.4 135.0 %copy-start.2 = (f32[3,1,256,512]{3,2,1,0:T(8,128)S(1)}, f32[3,1,256,512]{3,2,1,0:T(8,128)}, u32[]{:S(2)}) copy-start(f32[3,1,256,512]{3,2,1,0:T(8,128)} %copy-done.1) | copy-start | bytes 4718596
  707.4 135.0 %copy-start.17 = (f32[256,512]{1,0:T(8,128)S(1)}, f32[256,512]{1,0:T(8,128)}, u32[]{:S(2)}) copy-start(f32[256,512]{1,0:T(8,128)} %copy-done.16) | copy-start | bytes 1572868
  707.4 135.0 %copy-start.19 = (f32[512]{0:T(512)S(1)}, f32[512]{0:T(512)}, u32[]{:S(2)}) copy-start(f32[512]{0:T(512)} %param.9) | copy-start | bytes 6148
  707.4 112.5 %collective-permute-start.11 = (f32[2,256,512]{2,1,0:T(8,128)S(1)}, f32[2,256,512]{2,1,0:T(8,128)S(1)}, u32[]{:S(2)}, u32[]{:S(2)}) collective-permute-start(f32[2,256,512]{2,1,0:T(8,128)S(1)} %get-tuple-element.30), channel_id=1, source_target_pairs={{0,4},{1,5},{2,6},{3,7},{4,0},{5,1},{6,2},{7,3},{8,12},{9,13},{10,... | collective-permute-start | bytes 3145736 | tf_op jit(solution)/shard_map/ppermute | solution.py:9
  709.2 133.2 %collective-permute-start.12 = (f32[2,256,512]{2,1,0:T(8,128)S(1)}, f32[2,256,512]{2,1,0:T(8,128)S(1)}, u32[]{:S(2)}, u32[]{:S(2)}) collective-permute-start(f32[2,256,512]{2,1,0:T(8,128)S(1)} %get-tuple-element.31), channel_id=1, source_target_pairs={{0,4},{1,5},{2,6},{3,7},{4,0},{5,1},{6,2},{7,3},{8,12},{9,13},{10,... | collective-permute-start | bytes 3145736 | tf_op jit(solution)/shard_map/ppermute | solution.py:9
  850.5 554.3 %all-reduce.6.cloned.1.call-start = ((), (), s32[]{:S(2)}) async-start(), calls=%async_computation | async-start | bytes 16777216 | tf_op jit(solution)/shard_map/psum | solution.py:215
  1063.3 1.0 copy-start.9
  1065.6 6.5 copy-start.10
  1065.6 6.5 collective-permute-start.25
  1072.2 1.4 copy-start.18
Sparse Core Ops, SparseCore 0:
  850.6 212.7 all-reduce.7
  1065.9 338.8 all-reduce.5
